TPU v7x, 32 devices: a whole 2x2x4 slice. The times are simulated.
32 devices in a mesh: seq: 4 (over y, core), shard: 8 (over z, x).
Axes of the slice: x: 2, y: 2, z: 4, core: 2. Of those that a mesh axis runs over, the one named last changes fastest.
Arguments:
- hidden_in: bfloat16 [8, 1024, 1024], P('shard', 'seq'), may hold values from -6 to 6
- norm_gain: float32 [1024], replicated, may hold values from 0.5 to 1.5
- in_weight: bfloat16 [1024, 4384], P('shard'), may hold values from -0.1875 to 0.1875
- conv_weight: float32 [4, 2304], replicated, may hold values from -3 to 3
- conv_bias: float32 [2304], replicated, may hold values from -0.5 to 0.5
- dt_bias: float32 [32], replicated, may hold values from -4 to -1
- a_log: float32 [32], replicated, may hold values from -6 to 1
- skip: float32 [32], replicated, may hold values from 0.5 to 1.5
- inner_gain: float32 [2048], replicated, may hold values from 0.5 to 1.5
- out_weight: bfloat16 [2048, 1024], P('shard'), may hold values from -0.125 to 0.125
- out_grad: float32 [8, 1024, 1024], P('shard', 'seq'), may hold values from -6 to 6
Outputs:
- block_out: float32 [8, 1024, 1024], P('shard', 'seq')
- input_grad: float32 [8, 1024, 1024], P('shard', 'seq')
- norm_gain_grad: float32 [1024], replicated
- in_weight_grad: float32 [1024, 4384], P('shard')
- conv_weight_grad: float32 [4, 2304], replicated
- conv_bias_grad: float32 [2304], replicated
- dt_bias_grad: float32 [32], replicated
- a_log_grad: float32 [32], replicated
- skip_grad: float32 [32], replicated
- inner_gain_grad: float32 [2048], replicated
- out_weight_grad: float32 [2048, 1024], P('shard')
All inputs are finite; a program needn't handle non-finite values.
Results may differ from a plain program's by a relative error of at most 0.015.
Values may be sent and summed in bfloat16 or wider, within the bound.
No kernel may reach another device: no remote copies, remote signals or barrier semaphores. Data moves between devices by JAX's collectives and lax.ppermute only.
A program may use at most 128 MiB of HBM per device.

v0:
```python
import jax
import jax.numpy as jnp
from jax import lax
from jax.sharding import PartitionSpec as P

STATE = 128
GROUP = 256
norm_eps = 1e-05
highest = lax.Precision.HIGHEST


def passed_along(block, axis, distance):
    devices = range(lax.axis_size(axis))
    route = [(i - distance, i) for i in devices if i - distance in devices]
    return lax.ppermute(block, axis, route)


def contract_rows(left, right):
    return lax.dot_general(
        left, right, (((0,), (0,)), ((), ())), preferred_element_type=jnp.float32
    )


def contract_cols(left, right):
    return lax.dot_general(
        left, right, (((1,), (1,)), ((), ())), preferred_element_type=jnp.float32
    )


def section_one(conv_ext, dt_raw, conv_weight, conv_bias, dt_bias, a_log):
    rows = dt_raw.shape[0]
    width = conv_weight.shape[0]
    conv_out = conv_bias + conv_weight[0] * conv_ext[0:rows]
    for offset in range(1, width):
        conv_out = conv_out + conv_weight[offset] * conv_ext[offset : offset + rows]
    active = jax.nn.silu(conv_out)
    inner = conv_out.shape[1] - 2 * STATE
    x_heads = active[:, :inner]
    b_proj = active[:, inner : inner + STATE]
    c_proj = active[:, inner + STATE :]
    step_size = jax.nn.softplus(dt_raw + dt_bias)
    log_decay = -step_size * jnp.exp(a_log)
    return (x_heads, b_proj, c_proj, step_size, log_decay)


def ssd_groups(x_heads, b_proj, c_proj, step_size, log_decay, h_start):
    rows, heads = step_size.shape
    head_dim = x_heads.shape[1] // heads
    state_dim = b_proj.shape[1]
    blocks = rows // GROUP
    lower = jnp.arange(GROUP)[:, None] >= jnp.arange(GROUP)[None, :]
    mask = lower[None, :, :]

    def ssd_advance(state, pieces):
        x_blk, b_blk, c_blk, dt_blk, ld_blk = pieces
        cumul = jnp.cumsum(ld_blk, axis=0)
        cum_t = cumul.T
        spread = cum_t[:, :, None] - cum_t[:, None, :]
        kernel = jnp.where(mask, jnp.exp(jnp.where(mask, spread, 0.0)), 0.0)
        intersection = jnp.dot(c_blk, b_blk.T, precision=highest)
        kernel = kernel * intersection[None, :, :] * dt_blk.T[:, None, :]
        output = jnp.einsum("hts,shp->thp", kernel, x_blk, precision=highest)
        output = output + jnp.exp(cumul)[:, :, None] * jnp.einsum(
            "hpn,tn->thp", state, c_blk, precision=highest
        )
        weight_tail = jnp.exp(cumul[-1][None, :] - cumul) * dt_blk
        fresh = jnp.einsum("sh,shp,sn->hpn", weight_tail, x_blk, b_blk, precision=highest)
        state = jnp.exp(cumul[-1])[:, None, None] * state + fresh
        return (state, output)

    pieces = (
        x_heads.reshape(blocks, GROUP, heads, head_dim),
        b_proj.reshape(blocks, GROUP, state_dim),
        c_proj.reshape(blocks, GROUP, state_dim),
        step_size.reshape(blocks, GROUP, heads),
        log_decay.reshape(blocks, GROUP, heads),
    )
    h_end, outputs = lax.scan(ssd_advance, h_start, pieces)
    return (outputs.reshape(rows, heads * head_dim), h_end)


def end_states(x_heads, b_proj, step_size, log_decay, h_start):
    rows, heads = step_size.shape
    head_dim = x_heads.shape[1] // heads
    state_dim = b_proj.shape[1]
    blocks = rows // GROUP

    def end_advance(state, pieces):
        x_blk, b_blk, dt_blk, ld_blk = pieces
        cumul = jnp.cumsum(ld_blk, axis=0)
        weight_tail = jnp.exp(cumul[-1][None, :] - cumul) * dt_blk
        fresh = jnp.einsum("sh,shp,sn->hpn", weight_tail, x_blk, b_blk, precision=highest)
        return (jnp.exp(cumul[-1])[:, None, None] * state + fresh, None)

    pieces = (
        x_heads.reshape(blocks, GROUP, heads, head_dim),
        b_proj.reshape(blocks, GROUP, state_dim),
        step_size.reshape(blocks, GROUP, heads),
        log_decay.reshape(blocks, GROUP, heads),
    )
    h_end, unused = lax.scan(end_advance, h_start, pieces)
    return h_end


def section_three(ssd_out, x_heads, gate_z, skip, inner_gain):
    rows = ssd_out.shape[0]
    heads = skip.shape[0]
    mixed = ssd_out + (x_heads.reshape(rows, heads, -1) * skip[None, :, None]).reshape(rows, -1)
    gated_in = mixed * jax.nn.silu(gate_z)
    scale = lax.rsqrt(jnp.mean(gated_in * gated_in, axis=-1, keepdims=True) + norm_eps)
    return gated_in * scale * inner_gain


def body(
    hidden_in,
    norm_gain,
    in_weight,
    conv_weight,
    conv_bias,
    dt_bias,
    a_log,
    skip,
    inner_gain,
    out_weight,
    out_grad,
):
    tokens = hidden_in[0]
    tokens_f = tokens.astype(jnp.float32)
    cotan = out_grad[0]
    inner = inner_gain.shape[0]
    conv_dim = conv_bias.shape[0]
    width = conv_weight.shape[0]
    heads = dt_bias.shape[0]
    head_dim = inner // heads
    rows = tokens.shape[0]
    edge = rows - (width - 1)
    full_in, full_out = (
        lax.all_gather(in_weight, "shard", axis=0, tiled=True),
        lax.all_gather(out_weight, "shard", axis=0, tiled=True),
    )
    rstat = lax.rsqrt(jnp.mean(tokens_f * tokens_f, axis=-1, keepdims=True) + norm_eps)
    normed = (tokens_f * rstat * norm_gain).astype(jnp.bfloat16)
    projected = jnp.dot(normed, full_in, preferred_element_type=jnp.float32)
    gate_z = projected[:, :inner]
    conv_in = projected[:, inner : inner + conv_dim].astype(jnp.bfloat16)
    dt_raw = projected[:, inner + conv_dim :]
    before = passed_along(conv_in[edge:], "seq", 1)
    conv_ext = jnp.concatenate([before, conv_in], axis=0).astype(jnp.float32)
    firsts, back_one = jax.vjp(
        section_one, conv_ext, dt_raw, conv_weight, conv_bias, dt_bias, a_log
    )
    x_heads, b_proj, c_proj, step_size, log_decay = firsts
    h_zero = jnp.zeros((heads, head_dim, b_proj.shape[1]), jnp.float32)
    local_state = end_states(x_heads, b_proj, step_size, log_decay, h_zero)
    passing = jnp.exp(jnp.sum(log_decay, axis=0))

    def relay_step(turn, incoming):
        return passed_along(passing[:, None, None] * incoming + local_state, "seq", 1)

    h_in = lax.fori_loop(0, lax.axis_size("seq") - 1, relay_step, h_zero)

    def scan_states(x_one, b_one, c_one, s_one, l_one):
        return ssd_groups(x_one, b_one, c_one, s_one, l_one, h_in)

    (ssd_out, unused), back_two = jax.vjp(
        scan_states, x_heads, b_proj, c_proj, step_size, log_decay
    )
    growth = jnp.exp(jnp.cumsum(log_decay, axis=0))
    gated_pre, back_three = jax.vjp(section_three, ssd_out, x_heads, gate_z, skip, inner_gain)
    gated = gated_pre.astype(jnp.bfloat16)
    block_out = tokens_f + jnp.dot(gated, full_out, preferred_element_type=jnp.float32)
    cot_b = cotan.astype(jnp.bfloat16)
    d_gated = contract_cols(cot_b, lax.all_gather(out_weight, "shard", axis=0, tiled=True))
    d_ssd, d_x_three, d_gate, skip_grad, inner_gain_grad = back_three(d_gated)
    d_heads = d_ssd.reshape(rows, heads, head_dim)
    pulled = jnp.einsum("th,thp,tn->hpn", growth, d_heads, c_proj, precision=highest)

    def back_step(turn, later):
        return passed_along(
            (pulled + passing[:, None, None] * later).astype(jnp.bfloat16), "seq", -1
        ).astype(jnp.float32)

    h_grad = lax.fori_loop(0, lax.axis_size("seq") - 1, back_step, h_zero)
    d_x_two, d_b, d_c, d_step, d_log = back_two((d_ssd, h_grad))
    d_ext, d_dt_raw, conv_weight_part, conv_bias_part, dt_bias_part, a_log_part = back_one(
        (d_x_two + d_x_three, d_b, d_c, d_step, d_log)
    )
    returned = passed_along(d_ext[: width - 1], "seq", -1)
    d_conv = d_ext[width - 1 :]
    d_conv = jnp.concatenate([d_conv[:edge], d_conv[edge:] + returned], axis=0)
    d_proj = jnp.concatenate([d_gate, d_conv, d_dt_raw], axis=1).astype(jnp.bfloat16)
    d_normed = contract_cols(d_proj, lax.all_gather(in_weight, "shard", axis=0, tiled=True))
    norm_part = jnp.sum(d_normed * tokens_f * rstat, axis=0)
    scaled = norm_gain * d_normed
    input_grad = (
        cotan
        + rstat * scaled
        - tokens_f * rstat * rstat * rstat * jnp.mean(scaled * tokens_f, axis=-1, keepdims=True)
    )
    in_share = lax.psum_scatter(
        contract_rows(normed, d_proj).astype(jnp.bfloat16), "shard", scatter_dimension=0, tiled=True
    )
    out_share = lax.psum_scatter(
        contract_rows(gated, cot_b).astype(jnp.bfloat16), "shard", scatter_dimension=0, tiled=True
    )
    in_weight_grad, out_weight_grad = (
        lax.psum(in_share, "seq").astype(jnp.float32),
        lax.psum(out_share, "seq").astype(jnp.float32),
    )
    smalls = lax.psum(
        (
            norm_part,
            conv_weight_part,
            conv_bias_part,
            dt_bias_part,
            a_log_part,
            skip_grad,
            inner_gain_grad,
        ),
        ("seq", "shard"),
    )
    (
        norm_gain_grad,
        conv_weight_grad,
        conv_bias_grad,
        dt_bias_grad,
        a_log_grad,
        skip_total,
        gain_total,
    ) = smalls
    return (
        block_out[None],
        input_grad[None],
        norm_gain_grad,
        in_weight_grad,
        conv_weight_grad,
        conv_bias_grad,
        dt_bias_grad,
        a_log_grad,
        skip_total,
        gain_total,
        out_weight_grad,
    )


def solution(mesh):
    placed = (
        P("shard", "seq", None),
        P(),
        P("shard", None),
        P(),
        P(),
        P(),
        P(),
        P(),
        P(),
        P("shard", None),
        P("shard", "seq", None),
    )
    return jax.shard_map(
        body,
        mesh=mesh,
        in_specs=placed,
        out_specs=(
            P("shard", "seq", None),
            P("shard", "seq", None),
            P(),
            P("shard", None),
            P(),
            P(),
            P(),
            P(),
            P(),
            P(),
            P("shard", None),
        ),
        check_vma=False,
    )
```

profile of v0, /device:TPU:0, one launch (start us, length us, event | category | flops | bytes accessed | tf_op | source)
XLA Modules:
  0.0 726.6 jit_solution(14364811259111382184)
XLA Ops:
  13.8 131.1 %all-gather.3.cloned.1.call-done = bf16[1024,4384]{0,1:T(8,128)(2,1)} async-done(((bf16[128,4384]{0,1:T(8,128)(2,1)}), bf16[1024,4384]{0,1:T(8,128)(2,1)}) %all-gather.3.cloned.1.call-update) | async-done | bytes 8978448 | tf_op jit(solution)/shard_map/all_gather | solution.py:138
  144.9 6.3 fusion.107
  177.2 43.8 %while.17 = (s32[]{:T(128)}, f32[32,64,128]{2,1,0:T(8,128)S(1)}, f32[32]{0:T(128)S(1)}, f32[32,64,128]{2,1,0:T(8,128)}, s32[]{:T(128)}) while((s32[]{:T(128)}, f32[32,64,128]{2,1,0:T(8,128)S(1)}, f32[32]{0:T(128)S(1)}, f32[32,64,128]{2,1,0:T(8,128)}, s32[]{:T(128)}) %tuple.98), condition=%wide.region_5.6_spmd, body=%wide.region_4.5_spmd.sunk | while | flops 524290 | bytes 7340261 | solution.py:160
  188.3 11.5 %collective-permute-start = (f32[32,64,128]{2,1,0:T(8,128)}, f32[32,64,128]{2,1,0:T(8,128)S(1)}, u32[]{:S(2)}, u32[]{:S(2)}) collective-permute-start(f32[32,64,128]{2,1,0:T(8,128)} %multiply_add_fusion.7), channel_id=1, source_target_pairs={{0,8},{8,16},{16,24},{1,9},{9,17},{17,25},{2,10},{10,18},{18,26},{... | collective-permute-start | bytes 3145736 | tf_op jit(solution)/shard_map/while/body/eval_jaxpr/ppermute | solution.py:15
  204.6 13.9 %collective-permute-start = (f32[32,64,128]{2,1,0:T(8,128)}, f32[32,64,128]{2,1,0:T(8,128)S(1)}, u32[]{:S(2)}, u32[]{:S(2)}) collective-permute-start(f32[32,64,128]{2,1,0:T(8,128)} %multiply_add_fusion.7), channel_id=1, source_target_pairs={{0,8},{8,16},{16,24},{1,9},{9,17},{17,25},{2,10},{10,18},{18,26},{... | collective-permute-start | bytes 3145736 | tf_op jit(solution)/shard_map/while/body/eval_jaxpr/ppermute | solution.py:15
  223.9 11.9 %bitcast_add_fusion.1 = f32[256,32,64]{0,2,1:T(8,128)} fusion(f32[256,32,64]{0,2,1:T(8,128)S(1)} %fusion.78, f32[256,32,64]{0,2,1:T(8,128)S(1)} %bitcast.138, f32[32,256]{1,0:T(8,128)S(1)} %copy-done.48, f32[256,256]{1,0:T(8,128)S(1)} %copy-done.29, f32[32,256]{1,0:T(8,128)S(1)} %copy-done.50, pred[256,256]{1,0:T(8,128)(4,1)S(1)} %copy-done.44, ...), kind=kOutput, calls=%fused_computation.48 | convolution fusion | flops 1622147072 | bytes 6717440 | tf_op jit(solution)/shard_map/jvp()/while/body/eval_jaxpr/hts,shp->thp/dot_general | solution.py:62
  239.0 4.9 multiply_reduce_fusion.11
  245.0 5.6 multiply_reduce_fusion.7
  265.4 51.5 %while.18 = (s32[]{:T(128)}, f32[32,64,128]{2,1,0:T(8,128)}, f32[32]{0:T(128)}, f32[32,64,128]{2,1,0:T(8,128)}, s32[]{:T(128)}, /*index=5*/s32[]{:T(128)}) while((s32[]{:T(128)}, f32[32,64,128]{2,1,0:T(8,128)}, f32[32]{0:T(128)}, f32[32,64,128]{2,1,0:T(8,128)}, s32[]{:T(128)}, /*index=5*/s32[]{:T(128)}) %tuple.115), condition=%wide.region_10.11_spmd.clone, body=%wide.region_9.10_spmd.clone.sunk | while | flops 1310723 | bytes 6291703 | solution.py:183
  268.9 14.3 %collective-permute-done.1 = bf16[32,64,128]{2,1,0:T(8,128)(2,1)} collective-permute-done((bf16[32,64,128]{2,1,0:T(8,128)(2,1)}, bf16[32,64,128]{2,1,0:T(8,128)(2,1)}, u32[]{:S(2)}, u32[]{:S(2)}) %collective-permute-start.1) | collective-permute-done | bytes 524320 | tf_op jit(solution)/shard_map/while/body/eval_jaxpr/ppermute | solution.py:15
  289.2 10.2 %collective-permute-done.1 = bf16[32,64,128]{2,1,0:T(8,128)(2,1)} collective-permute-done((bf16[32,64,128]{2,1,0:T(8,128)(2,1)}, bf16[32,64,128]{2,1,0:T(8,128)(2,1)}, u32[]{:S(2)}, u32[]{:S(2)}) %collective-permute-start.1) | collective-permute-done | bytes 524320 | tf_op jit(solution)/shard_map/while/body/eval_jaxpr/ppermute | solution.py:15
  305.3 9.5 %collective-permute-done.1 = bf16[32,64,128]{2,1,0:T(8,128)(2,1)} collective-permute-done((bf16[32,64,128]{2,1,0:T(8,128)(2,1)}, bf16[32,64,128]{2,1,0:T(8,128)(2,1)}, u32[]{:S(2)}, u32[]{:S(2)}) %collective-permute-start.1) | collective-permute-done | bytes 524320 | tf_op jit(solution)/shard_map/while/body/eval_jaxpr/ppermute | solution.py:15
  326.5 14.6 %fusion.10 = (f32[32,256]{1,0:T(8,128)}, f32[32,256]{1,0:T(8,128)}, f32[32,256]{1,0:T(8,128)}, f32[256,256]{1,0:T(8,128)}) fusion(f32[32,256]{1,0:T(8,128)S(1)} %copy-done.49, f32[256,256]{1,0:T(8,128)S(1)} %copy-done.30, f32[32,256]{1,0:T(8,128)S(1)} %copy-done.51, pred[256,256]{1,0:T(8,128)(4,1)S(1)} %copy-done.45, f32[32,64,256]{2,1,0:T(8,128)S(1)} %bitcast.142, ...), kind=kOutput, calls=%fused_computation.15 | convolution fusion | flops 1641979904 | bytes 4947968 | tf_op jit(solution)/shard_map/transpose(jvp())/while/body/eval_jaxpr/hts,shp->thp/dot_general | solution.py:62
  341.1 8.8 %bitcast_add_fusion = f32[256,32,64]{0,2,1:T(8,128)} fusion(f32[256,32,64]{0,2,1:T(8,128)S(1)} %get-tuple-element.505, f32[32,64,256]{2,1,0:T(8,128)S(1)} %bitcast.143, f32[32,256]{1,0:T(8,128)S(1)} %copy-done.49, f32[256,256]{1,0:T(8,128)S(1)} %copy-done.30, f32[32,256]{1,0:T(8,128)S(1)} %copy-done.51, pred[256,256]{1,0:T(8,128)(4,1)S(1)} %copy-done.45, ...), kind=kOutput, calls=%fused_computation.47 | convolution fusion | flops 1622147072 | bytes 6717440 | tf_op jit(solution)/shard_map/transpose(jvp())/while/body/eval_jaxpr/hts,shp->thp/dot_general | solution.py:62
  352.8 5.8 fusion.106
  361.5 5.2 convolution_bitcast_fusion
  387.6 5.8 collective-permute-done.3
  394.3 6.1 convolution_convert_fusion
  400.5 11.8 %copy.162 = bf16[1024,4384]{1,0:T(8,128)(2,1)} copy(bf16[1024,4384]{0,1:T(8,128)(2,1)} %convolution_convert_fusion) | data formatting | bytes 17956864
  418.4 4.7 fusion.43
  423.1 149.3 %reduce-scatter.7.cloned.1.call-done = bf16[128,4384]{1,0:T(8,128)(2,1)} async-done(((bf16[1024,4384]{1,0:T(8,128)(2,1)}), bf16[128,4384]{1,0:T(8,128)(2,1)}) %reduce-scatter.7.cloned.1.call-update) | async-done | bytes 1122320
  574.8 88.6 %reduce-scatter.5.cloned.1.call-done = bf16[256,1024]{1,0:T(8,128)(2,1)} async-done(((bf16[2048,1024]{1,0:T(8,128)(2,1)}), bf16[256,1024]{1,0:T(8,128)(2,1)}) %reduce-scatter.5.cloned.1.call-update) | async-done | bytes 524304 | tf_op jit(solution)/shard_map/reduce_scatter | solution.py:203
  663.4 7.6 %fusion.57 = (f32[1024]{0:T(1024)S(1)}, f32[256]{0:T(256)S(1)}, f32[256,1024]{1,0:T(8,128)}) fusion(bf16[1,256,1024]{2,1,0:T(8,128)(2,1)S(1)} %copy-done.23, f32[256]{0:T(256)S(1)} %copy-done.64, f32[1024]{0:T(1024)S(1)} %copy-done.57, bf16[1024,4384]{0,1:T(8,128)(2,1)} %all-gather.3.cloned.1.call-done, bf16[256,32]{1,0:T(8,128)(2,1)S(1)} %get-tuple-element.482, ...), kind=kOutput, calls=%fused_computation.92 | convolution fusion | flops 2309290752 | bytes 12806144 | tf_op jit(solution)/shard_map/dot_general | solution.py:25
  671.0 42.5 %all-reduce.13 = (f32[1024]{0:T(1024)}, f32[4,2304]{1,0:T(4,128)}, f32[2304]{0:T(1024)}, f32[32]{0:T(128)}, f32[32]{0:T(128)}, /*index=5*/f32[32]{0:T(128)}, f32[2048]{0:T(1024)}) all-reduce(f32[1024]{0:T(1024)S(1)} %get-tuple-element.448, f32[4,2304]{1,0:T(4,128)S(1)} %pad_add_fusion.2, ...), channel_id=1, replica_groups=mesh['seq'=4,'shard'=8] {'seq','shard'}, use_global_device_ids=true, to_apply=%region_21.22 | all-reduce | flops 14688 | bytes 117504 | tf_op jit(solution)/shard_map/psum | solution.py:210
  (259 shorter events, 141.9 us)
Async XLA Ops:
  7.2 137.8 %copy-start.21 = (bf16[1,256,1024]{2,1,0:T(8,128)(2,1)S(1)}, bf16[1,256,1024]{2,1,0:T(8,128)(2,1)}, u32[]{:S(2)}) copy-start(bf16[1,256,1024]{2,1,0:T(8,128)(2,1)} %param.15) | copy-start | bytes 1572868
  7.2 137.8 %copy-start.56 = (f32[1024]{0:T(1024)S(1)}, f32[1024]{0:T(1024)}, u32[]{:S(2)}) copy-start(f32[1024]{0:T(1024)} %param.16) | copy-start | bytes 12292
  7.2 137.7 %all-gather.3.cloned.1.call-start = ((), (), s32[]{:S(2)}) async-start(), calls=%async_computation.2 | async-start | bytes 10100736 | tf_op jit(solution)/shard_map/all_gather | solution.py:138
  7.9 237.0 %all-gather.5.cloned.1.call-start = ((), (), s32[]{:S(2)}) async-start(), calls=%async_computation.3 | async-start | bytes 4718592 | tf_op jit(solution)/shard_map/all_gather | solution.py:139
  8.7 563.7 %reduce-scatter.7.cloned.1.call-start = ((), (), s32[]{:S(2)}) async-start(), calls=%async_computation.5 | async-start | bytes 10321920
  9.4 143.3 %copy-start.67 = (f32[32]{0:T(128)}, f32[32]{0:T(128)S(1)}, u32[]{:S(2)}) copy-start(f32[32]{0:T(128)S(1)} %exp.120) | copy-start | bytes 388
  12.5 149.3 %copy-start.34 = (f32[2304]{0:T(1024)}, f32[2304]{0:T(1024)S(1)}, u32[]{:S(2)}) copy-start(f32[2304]{0:T(1024)S(1)} %get-tuple-element.450) | copy-start | bytes 27652
  12.5 149.3 %copy-start.36 = (f32[2304]{0:T(1024)}, f32[2304]{0:T(1024)S(1)}, u32[]{:S(2)}) copy-start(f32[2304]{0:T(1024)S(1)} %get-tuple-element.451) | copy-start | bytes 27652
  12.5 149.3 %copy-start.38 = (f32[2304]{0:T(1024)}, f32[2304]{0:T(1024)S(1)}, u32[]{:S(2)}) copy-start(f32[2304]{0:T(1024)S(1)} %get-tuple-element.452) | copy-start | bytes 27652
  12.5 149.3 %copy-start.40 = (f32[2304]{0:T(1024)}, f32[2304]{0:T(1024)S(1)}, u32[]{:S(2)}) copy-start(f32[2304]{0:T(1024)S(1)} %get-tuple-element.453) | copy-start | bytes 27652
  13.8 137.4 %copy-start.63 = (f32[256]{0:T(256)}, f32[256]{0:T(256)S(1)}, u32[]{:S(2)}) copy-start(f32[256]{0:T(256)S(1)} %add_rsqrt_fusion) | copy-start | bytes 3076
  13.8 139.5 %copy-start.58 = (f32[32]{0:T(128)S(1)}, f32[32]{0:T(128)}, u32[]{:S(2)}) copy-start(f32[32]{0:T(128)} %param.20) | copy-start | bytes 388
  151.2 9.0 %collective-permute-start.2 = (bf16[3,2304]{1,0:T(4,128)(2,1)S(1)}, bf16[3,2304]{1,0:T(4,128)(2,1)S(1)}, u32[]{:S(2)}, u32[]{:S(2)}) collective-permute-start(bf16[3,2304]{1,0:T(4,128)(2,1)S(1)} %slice.123), channel_id=1, source_target_pairs={{0,8},{8,16},{16,24},{1,9},{9,17},{17,25},{2,10},{10,18},{18,26},{... | collective-permute-start | bytes 41480 | tf_op jit(solution)/shard_map/ppermute | solution.py:15
  179.6 6.3 collective-permute-start
  188.3 13.9 %collective-permute-start = (f32[32,64,128]{2,1,0:T(8,128)}, f32[32,64,128]{2,1,0:T(8,128)S(1)}, u32[]{:S(2)}, u32[]{:S(2)}) collective-permute-start(f32[32,64,128]{2,1,0:T(8,128)} %multiply_add_fusion.7), channel_id=1, source_target_pairs={{0,8},{8,16},{16,24},{1,9},{9,17},{17,25},{2,10},{10,18},{18,26},{... | collective-permute-start | bytes 3145736 | tf_op jit(solution)/shard_map/while/body/eval_jaxpr/ppermute | solution.py:15
  204.6 16.3 %collective-permute-start = (f32[32,64,128]{2,1,0:T(8,128)}, f32[32,64,128]{2,1,0:T(8,128)S(1)}, u32[]{:S(2)}, u32[]{:S(2)}) collective-permute-start(f32[32,64,128]{2,1,0:T(8,128)} %multiply_add_fusion.7), channel_id=1, source_target_pairs={{0,8},{8,16},{16,24},{1,9},{9,17},{17,25},{2,10},{10,18},{18,26},{... | collective-permute-start | bytes 3145736 | tf_op jit(solution)/shard_map/while/body/eval_jaxpr/ppermute | solution.py:15
  267.6 15.6 %collective-permute-start.1 = (bf16[32,64,128]{2,1,0:T(8,128)(2,1)}, bf16[32,64,128]{2,1,0:T(8,128)(2,1)}, u32[]{:S(2)}, u32[]{:S(2)}) collective-permute-start(bf16[32,64,128]{2,1,0:T(8,128)(2,1)} %fusion.132), channel_id=1, source_target_pairs={{8,0},{16,8},{24,16},{9,1},{17,9},{25,17},{10,2},{18,10},{26,18},{... | collective-permute-start | bytes 1572872 | tf_op jit(solution)/shard_map/while/body/eval_jaxpr/ppermute | solution.py:15
  287.9 11.4 %collective-permute-start.1 = (bf16[32,64,128]{2,1,0:T(8,128)(2,1)}, bf16[32,64,128]{2,1,0:T(8,128)(2,1)}, u32[]{:S(2)}, u32[]{:S(2)}) collective-permute-start(bf16[32,64,128]{2,1,0:T(8,128)(2,1)} %fusion.132), channel_id=1, source_target_pairs={{8,0},{16,8},{24,16},{9,1},{17,9},{25,17},{10,2},{18,10},{26,18},{... | collective-permute-start | bytes 1572872 | tf_op jit(solution)/shard_map/while/body/eval_jaxpr/ppermute | solution.py:15
  304.0 10.8 %collective-permute-start.1 = (bf16[32,64,128]{2,1,0:T(8,128)(2,1)}, bf16[32,64,128]{2,1,0:T(8,128)(2,1)}, u32[]{:S(2)}, u32[]{:S(2)}) collective-permute-start(bf16[32,64,128]{2,1,0:T(8,128)(2,1)} %fusion.132), channel_id=1, source_target_pairs={{8,0},{16,8},{24,16},{9,1},{17,9},{25,17},{10,2},{18,10},{26,18},{... | collective-permute-start | bytes 1572872 | tf_op jit(solution)/shard_map/while/body/eval_jaxpr/ppermute | solution.py:15
  383.4 9.9 %collective-permute-start.3 = (f32[3,2304]{1,0:T(4,128)S(1)}, f32[3,2304]{1,0:T(4,128)S(1)}, u32[]{:S(2)}, u32[]{:S(2)}) collective-permute-start(f32[3,2304]{1,0:T(4,128)S(1)} %pad_add_fusion.1), channel_id=1, source_target_pairs={{8,0},{16,8},{24,16},{9,1},{17,9},{25,17},{10,2},{18,10},{26,18},{... | collective-permute-start | bytes 82952 | tf_op jit(solution)/shard_map/ppermute | solution.py:15
  412.3 251.1 %reduce-scatter.5.cloned.1.call-start = ((), (), s32[]{:S(2)}) async-start(), calls=%async_computation.4 | async-start | bytes 4718592 | tf_op jit(solution)/shard_map/reduce_scatter | solution.py:203
  417.5 298.5 %all-reduce.17.cloned.1.call-start = ((), (), s32[]{:S(2)}) async-start(), calls=%async_computation.6 | async-start | bytes 3293184 | tf_op jit(solution)/shard_map/psum | solution.py:207
  423.1 240.3 %copy-start.23 = (bf16[1,256,1024]{2,1,0:T(8,128)(2,1)S(1)}, bf16[1,256,1024]{2,1,0:T(8,128)(2,1)}, u32[]{:S(2)}) copy-start(bf16[1,256,1024]{2,1,0:T(8,128)(2,1)} %param.15) | copy-start | bytes 1572868
  423.1 240.3 %copy-start.25 = (bf16[253,2304]{1,0:T(8,128)(2,1)S(1)}, bf16[253,2304]{1,0:T(8,128)(2,1)}, u32[]{:S(2)}) copy-start(bf16[253,2304]{1,0:T(8,128)(2,1)} %copy-done.24) | copy-start | bytes 3497476
  (60 other events, 255.0 us)
Sparse Core Ops, SparseCore 0:
  10.1 134.8 all-gather.2
  147.1 70.9 all-gather.4
  412.4 159.9 reduce-scatter.6
  575.9 87.3 reduce-scatter.4
  666.2 45.0 all-reduce.16
where the time goes:
time: 731 us; the launch traced here: 727 us
  waiting for transfers between devices  417 us (57%)
  matrix products  98 us (13%)
  other arithmetic  67.7 us (9%)
  local copies, waits for them, and re-layouts  49.9 us (7%)
  blocking collectives  42.5 us (6%)
  starting transfers between devices  36.2 us (5%)
  between operations  14.9 us (2%)
    unnamed x6, waiting for transfers between devices  151 us
    all_gather x1, waiting for transfers between devices, body(): lax.all_gather(in_weight, 'shard', axis=0, tiled=True)  131 us
    reduce_scatter x1, waiting for transfers between devices, body(): lax.psum_scatter(contract_rows(gated, cot_b).astype(jnp.bfloat16), 'shard...  88.6 us
    ppermute x8, waiting for transfers between devices, passed_along(): return lax.ppermute(block, axis, route)  46.9 us
    psum x1, blocking collectives, body(): lax.psum((norm_part, conv_weight_part, conv_bias_part, dt_bias_part, a_lo...  42.5 us
    ppermute x8, starting transfers between devices, passed_along(): return lax.ppermute(block, axis, route)  36 us
    dot_general x3, matrix products, ssd_advance(): output = jnp.einsum('hts,shp->thp', kernel, x_blk, precision=highest)  35.2 us
    unnamed x144, local copies, waits for them, and re-layouts  22.8 us
  transfers between devices with their start and end apart: 13, of which 10 were waited for; matrix products, arithmetic and copies ran while one was open for 12% of the time, Pallas kernels for 0%

commit v1 on v0

--- a/solution.py
+++ b/solution.py
@@ -208,16 +208,19 @@
         lax.psum(out_share, "seq").astype(jnp.float32),
     )
     smalls = lax.psum(
-        (
-            norm_part,
-            conv_weight_part,
-            conv_bias_part,
-            dt_bias_part,
-            a_log_part,
-            skip_grad,
-            inner_gain_grad,
+        lax.psum(
+            (
+                norm_part,
+                conv_weight_part,
+                conv_bias_part,
+                dt_bias_part,
+                a_log_part,
+                skip_grad,
+                inner_gain_grad,
+            ),
+            "shard",
         ),
-        ("seq", "shard"),
+        "seq",
     )
     (
         norm_gain_grad,

time: 731 us -> 736 us (level)
    psum x0 -> x1, blocking collectives: none -> 11.3 us  [body(): lax.psum(lax.psum((norm_part, conv_weight_part, conv_bias_part, dt_bias_p...]
where the time goes in v1:
time: 736 us; the launch traced here: 732 us
  waiting for transfers between devices  417 us (57%)
  matrix products  98 us (13%)
  other arithmetic  67.7 us (9%)
  local copies, waits for them, and re-layouts  49.9 us (7%)
  blocking collectives  47.6 us (6%)
  starting transfers between devices  36.2 us (5%)
  between operations  14.9 us (2%)
    unnamed x6, waiting for transfers between devices  151 us
    all_gather x1, waiting for transfers between devices, body(): lax.all_gather(in_weight, 'shard', axis=0, tiled=True)  131 us
    reduce_scatter x1, waiting for transfers between devices, body(): lax.psum_scatter(contract_rows(gated, cot_b).astype(jnp.bfloat16), 'shard...  88.6 us
    ppermute x8, waiting for transfers between devices, passed_along(): return lax.ppermute(block, axis, route)  46.9 us
    psum x1, blocking collectives, body(): lax.psum((norm_part, conv_weight_part, conv_bias_part, dt_bias_part, a_lo...  36.3 us
    ppermute x8, starting transfers between devices, passed_along(): return lax.ppermute(block, axis, route)  36 us
    dot_general x3, matrix products, ssd_advance(): output = jnp.einsum('hts,shp->thp', kernel, x_blk, precision=highest)  35.2 us
    unnamed x144, local copies, waits for them, and re-layouts  22.8 us
  transfers between devices with their start and end apart: 13, of which 10 were waited for; matrix products, arithmetic and copies ran while one was open for 12% of the time, Pallas kernels for 0%

profile of v1, /device:TPU:0, one launch (start us, length us, event | category | flops | bytes accessed | tf_op | source)
XLA Modules:
  0.0 731.8 jit_solution(17844243235737477580)
XLA Ops:
  13.8 131.1 %all-gather.3.cloned.1.call-done = bf16[1024,4384]{0,1:T(8,128)(2,1)} async-done(((bf16[128,4384]{0,1:T(8,128)(2,1)}), bf16[1024,4384]{0,1:T(8,128)(2,1)}) %all-gather.3.cloned.1.call-update) | async-done | bytes 8978448 | tf_op jit(solution)/shard_map/all_gather | solution.py:138
  144.9 6.3 fusion.107
  177.2 43.8 %while.17 = (s32[]{:T(128)}, f32[32,64,128]{2,1,0:T(8,128)S(1)}, f32[32]{0:T(128)S(1)}, f32[32,64,128]{2,1,0:T(8,128)}, s32[]{:T(128)}) while((s32[]{:T(128)}, f32[32,64,128]{2,1,0:T(8,128)S(1)}, f32[32]{0:T(128)S(1)}, f32[32,64,128]{2,1,0:T(8,128)}, s32[]{:T(128)}) %tuple.98), condition=%wide.region_5.6_spmd, body=%wide.region_4.5_spmd.sunk | while | flops 524290 | bytes 7340261 | solution.py:160
  188.3 11.5 %collective-permute-start = (f32[32,64,128]{2,1,0:T(8,128)}, f32[32,64,128]{2,1,0:T(8,128)S(1)}, u32[]{:S(2)}, u32[]{:S(2)}) collective-permute-start(f32[32,64,128]{2,1,0:T(8,128)} %multiply_add_fusion.7), channel_id=1, source_target_pairs={{0,8},{8,16},{16,24},{1,9},{9,17},{17,25},{2,10},{10,18},{18,26},{... | collective-permute-start | bytes 3145736 | tf_op jit(solution)/shard_map/while/body/eval_jaxpr/ppermute | solution.py:15
  204.6 13.9 %collective-permute-start = (f32[32,64,128]{2,1,0:T(8,128)}, f32[32,64,128]{2,1,0:T(8,128)S(1)}, u32[]{:S(2)}, u32[]{:S(2)}) collective-permute-start(f32[32,64,128]{2,1,0:T(8,128)} %multiply_add_fusion.7), channel_id=1, source_target_pairs={{0,8},{8,16},{16,24},{1,9},{9,17},{17,25},{2,10},{10,18},{18,26},{... | collective-permute-start | bytes 3145736 | tf_op jit(solution)/shard_map/while/body/eval_jaxpr/ppermute | solution.py:15
  223.9 11.9 %bitcast_add_fusion.1 = f32[256,32,64]{0,2,1:T(8,128)} fusion(f32[256,32,64]{0,2,1:T(8,128)S(1)} %fusion.78, f32[256,32,64]{0,2,1:T(8,128)S(1)} %bitcast.138, f32[32,256]{1,0:T(8,128)S(1)} %copy-done.48, f32[256,256]{1,0:T(8,128)S(1)} %copy-done.29, f32[32,256]{1,0:T(8,128)S(1)} %copy-done.50, pred[256,256]{1,0:T(8,128)(4,1)S(1)} %copy-done.44, ...), kind=kOutput, calls=%fused_computation.48 | convolution fusion | flops 1622147072 | bytes 6717440 | tf_op jit(solution)/shard_map/jvp()/while/body/eval_jaxpr/hts,shp->thp/dot_general | solution.py:62
  239.0 4.9 multiply_reduce_fusion.11
  245.0 5.6 multiply_reduce_fusion.7
  265.4 51.5 %while.18 = (s32[]{:T(128)}, f32[32,64,128]{2,1,0:T(8,128)}, f32[32]{0:T(128)}, f32[32,64,128]{2,1,0:T(8,128)}, s32[]{:T(128)}, /*index=5*/s32[]{:T(128)}) while((s32[]{:T(128)}, f32[32,64,128]{2,1,0:T(8,128)}, f32[32]{0:T(128)}, f32[32,64,128]{2,1,0:T(8,128)}, s32[]{:T(128)}, /*index=5*/s32[]{:T(128)}) %tuple.115), condition=%wide.region_10.11_spmd.clone, body=%wide.region_9.10_spmd.clone.sunk | while | flops 1310723 | bytes 6291703 | solution.py:183
  268.9 14.3 %collective-permute-done.1 = bf16[32,64,128]{2,1,0:T(8,128)(2,1)} collective-permute-done((bf16[32,64,128]{2,1,0:T(8,128)(2,1)}, bf16[32,64,128]{2,1,0:T(8,128)(2,1)}, u32[]{:S(2)}, u32[]{:S(2)}) %collective-permute-start.1) | collective-permute-done | bytes 524320 | tf_op jit(solution)/shard_map/while/body/eval_jaxpr/ppermute | solution.py:15
  289.2 10.2 %collective-permute-done.1 = bf16[32,64,128]{2,1,0:T(8,128)(2,1)} collective-permute-done((bf16[32,64,128]{2,1,0:T(8,128)(2,1)}, bf16[32,64,128]{2,1,0:T(8,128)(2,1)}, u32[]{:S(2)}, u32[]{:S(2)}) %collective-permute-start.1) | collective-permute-done | bytes 524320 | tf_op jit(solution)/shard_map/while/body/eval_jaxpr/ppermute | solution.py:15
  305.3 9.5 %collective-permute-done.1 = bf16[32,64,128]{2,1,0:T(8,128)(2,1)} collective-permute-done((bf16[32,64,128]{2,1,0:T(8,128)(2,1)}, bf16[32,64,128]{2,1,0:T(8,128)(2,1)}, u32[]{:S(2)}, u32[]{:S(2)}) %collective-permute-start.1) | collective-permute-done | bytes 524320 | tf_op jit(solution)/shard_map/while/body/eval_jaxpr/ppermute | solution.py:15
  326.5 14.6 %fusion.10 = (f32[32,256]{1,0:T(8,128)}, f32[32,256]{1,0:T(8,128)}, f32[32,256]{1,0:T(8,128)}, f32[256,256]{1,0:T(8,128)}) fusion(f32[32,256]{1,0:T(8,128)S(1)} %copy-done.49, f32[256,256]{1,0:T(8,128)S(1)} %copy-done.30, f32[32,256]{1,0:T(8,128)S(1)} %copy-done.51, pred[256,256]{1,0:T(8,128)(4,1)S(1)} %copy-done.45, f32[32,64,256]{2,1,0:T(8,128)S(1)} %bitcast.142, ...), kind=kOutput, calls=%fused_computation.15 | convolution fusion | flops 1641979904 | bytes 4947968 | tf_op jit(solution)/shard_map/transpose(jvp())/while/body/eval_jaxpr/hts,shp->thp/dot_general | solution.py:62
  341.1 8.8 %bitcast_add_fusion = f32[256,32,64]{0,2,1:T(8,128)} fusion(f32[256,32,64]{0,2,1:T(8,128)S(1)} %get-tuple-element.512, f32[32,64,256]{2,1,0:T(8,128)S(1)} %bitcast.143, f32[32,256]{1,0:T(8,128)S(1)} %copy-done.49, f32[256,256]{1,0:T(8,128)S(1)} %copy-done.30, f32[32,256]{1,0:T(8,128)S(1)} %copy-done.51, pred[256,256]{1,0:T(8,128)(4,1)S(1)} %copy-done.45, ...), kind=kOutput, calls=%fused_computation.47 | convolution fusion | flops 1622147072 | bytes 6717440 | tf_op jit(solution)/shard_map/transpose(jvp())/while/body/eval_jaxpr/hts,shp->thp/dot_general | solution.py:62
  352.8 5.8 fusion.106
  361.5 5.2 convolution_bitcast_fusion
  387.6 5.8 collective-permute-done.3
  394.3 6.1 convolution_convert_fusion
  400.5 11.8 %copy.162 = bf16[1024,4384]{1,0:T(8,128)(2,1)} copy(bf16[1024,4384]{0,1:T(8,128)(2,1)} %convolution_convert_fusion) | data formatting | bytes 17956864
  423.1 149.3 %reduce-scatter.7.cloned.1.call-done = bf16[128,4384]{1,0:T(8,128)(2,1)} async-done(((bf16[1024,4384]{1,0:T(8,128)(2,1)}), bf16[128,4384]{1,0:T(8,128)(2,1)}) %reduce-scatter.7.cloned.1.call-update) | async-done | bytes 1122320
  574.8 88.6 %reduce-scatter.5.cloned.1.call-done = bf16[256,1024]{1,0:T(8,128)(2,1)} async-done(((bf16[2048,1024]{1,0:T(8,128)(2,1)}), bf16[256,1024]{1,0:T(8,128)(2,1)}) %reduce-scatter.5.cloned.1.call-update) | async-done | bytes 524304 | tf_op jit(solution)/shard_map/reduce_scatter | solution.py:203
  663.4 7.6 %fusion.57 = (f32[1024]{0:T(1024)S(1)}, f32[256]{0:T(256)S(1)}, f32[256,1024]{1,0:T(8,128)}) fusion(bf16[1,256,1024]{2,1,0:T(8,128)(2,1)S(1)} %copy-done.23, f32[256]{0:T(256)S(1)} %copy-done.64, f32[1024]{0:T(1024)S(1)} %copy-done.57, bf16[1024,4384]{0,1:T(8,128)(2,1)} %all-gather.3.cloned.1.call-done, bf16[256,32]{1,0:T(8,128)(2,1)S(1)} %get-tuple-element.489, ...), kind=kOutput, calls=%fused_computation.92 | convolution fusion | flops 2309290752 | bytes 12806144 | tf_op jit(solution)/shard_map/dot_general | solution.py:25
  671.0 36.3 %all-reduce.13 = (f32[1024]{0:T(1024)S(1)}, f32[4,2304]{1,0:T(4,128)S(1)}, f32[2304]{0:T(1024)S(1)}, f32[32]{0:T(128)S(1)}, f32[32]{0:T(128)S(1)}, /*index=5*/f32[32]{0:T(128)S(1)}, f32[2048]{0:T(1024)S(1)}) all-reduce(f32[1024]{0:T(1024)S(1)} %get-tuple-element.448, ...), channel_id=1, replica_groups=mesh['seq'=4,'shard'=8] {'shard'}, use_global_device_ids=true, to_apply=%region_21.22 | all-reduce | flops 14688 | bytes 117504 | tf_op jit(solution)/shard_map/psum | solution.py:211
  707.3 11.3 %all-reduce.14 = (f32[1024]{0:T(1024)}, f32[4,2304]{1,0:T(4,128)}, f32[2304]{0:T(1024)}, f32[32]{0:T(128)}, f32[32]{0:T(128)}, /*index=5*/f32[32]{0:T(128)}, f32[2048]{0:T(1024)}) all-reduce(f32[1024]{0:T(1024)S(1)} %get-tuple-element.470, f32[4,2304]{1,0:T(4,128)S(1)} %get-tuple-element.471, ...), channel_id=1, replica_groups=mesh['seq'=4,'shard'=8] {'seq'}, use_global_device_ids=true, to_apply=%region_22.23 | all-reduce | flops 14688 | bytes 117504 | tf_op jit(solution)/shard_map/psum | solution.py:210
  (260 shorter events, 146.6 us)
Async XLA Ops:
  7.2 137.8 %copy-start.21 = (bf16[1,256,1024]{2,1,0:T(8,128)(2,1)S(1)}, bf16[1,256,1024]{2,1,0:T(8,128)(2,1)}, u32[]{:S(2)}) copy-start(bf16[1,256,1024]{2,1,0:T(8,128)(2,1)} %param.15) | copy-start | bytes 1572868
  7.2 137.8 %copy-start.56 = (f32[1024]{0:T(1024)S(1)}, f32[1024]{0:T(1024)}, u32[]{:S(2)}) copy-start(f32[1024]{0:T(1024)} %param.16) | copy-start | bytes 12292
  7.2 137.7 %all-gather.3.cloned.1.call-start = ((), (), s32[]{:S(2)}) async-start(), calls=%async_computation.2 | async-start | bytes 10100736 | tf_op jit(solution)/shard_map/all_gather | solution.py:138
  7.9 237.0 %all-gather.5.cloned.1.call-start = ((), (), s32[]{:S(2)}) async-start(), calls=%async_computation.3 | async-start | bytes 4718592 | tf_op jit(solution)/shard_map/all_gather | solution.py:139
  8.7 563.7 %reduce-scatter.7.cloned.1.call-start = ((), (), s32[]{:S(2)}) async-start(), calls=%async_computation.5 | async-start | bytes 10321920
  9.4 143.3 %copy-start.67 = (f32[32]{0:T(128)}, f32[32]{0:T(128)S(1)}, u32[]{:S(2)}) copy-start(f32[32]{0:T(128)S(1)} %exp.120) | copy-start | bytes 388
  12.5 149.3 %copy-start.34 = (f32[2304]{0:T(1024)}, f32[2304]{0:T(1024)S(1)}, u32[]{:S(2)}) copy-start(f32[2304]{0:T(1024)S(1)} %get-tuple-element.450) | copy-start | bytes 27652
  12.5 149.3 %copy-start.36 = (f32[2304]{0:T(1024)}, f32[2304]{0:T(1024)S(1)}, u32[]{:S(2)}) copy-start(f32[2304]{0:T(1024)S(1)} %get-tuple-element.451) | copy-start | bytes 27652
  12.5 149.3 %copy-start.38 = (f32[2304]{0:T(1024)}, f32[2304]{0:T(1024)S(1)}, u32[]{:S(2)}) copy-start(f32[2304]{0:T(1024)S(1)} %get-tuple-element.452) | copy-start | bytes 27652
  12.5 149.3 %copy-start.40 = (f32[2304]{0:T(1024)}, f32[2304]{0:T(1024)S(1)}, u32[]{:S(2)}) copy-start(f32[2304]{0:T(1024)S(1)} %get-tuple-element.453) | copy-start | bytes 27652
  13.8 137.4 %copy-start.63 = (f32[256]{0:T(256)}, f32[256]{0:T(256)S(1)}, u32[]{:S(2)}) copy-start(f32[256]{0:T(256)S(1)} %add_rsqrt_fusion) | copy-start | bytes 3076
  13.8 139.5 %copy-start.58 = (f32[32]{0:T(128)S(1)}, f32[32]{0:T(128)}, u32[]{:S(2)}) copy-start(f32[32]{0:T(128)} %param.20) | copy-start | bytes 388
  151.2 9.0 %collective-permute-start.2 = (bf16[3,2304]{1,0:T(4,128)(2,1)S(1)}, bf16[3,2304]{1,0:T(4,128)(2,1)S(1)}, u32[]{:S(2)}, u32[]{:S(2)}) collective-permute-start(bf16[3,2304]{1,0:T(4,128)(2,1)S(1)} %slice.123), channel_id=1, source_target_pairs={{0,8},{8,16},{16,24},{1,9},{9,17},{17,25},{2,10},{10,18},{18,26},{... | collective-permute-start | bytes 41480 | tf_op jit(solution)/shard_map/ppermute | solution.py:15
  179.6 6.3 collective-permute-start
  188.3 13.9 %collective-permute-start = (f32[32,64,128]{2,1,0:T(8,128)}, f32[32,64,128]{2,1,0:T(8,128)S(1)}, u32[]{:S(2)}, u32[]{:S(2)}) collective-permute-start(f32[32,64,128]{2,1,0:T(8,128)} %multiply_add_fusion.7), channel_id=1, source_target_pairs={{0,8},{8,16},{16,24},{1,9},{9,17},{17,25},{2,10},{10,18},{18,26},{... | collective-permute-start | bytes 3145736 | tf_op jit(solution)/shard_map/while/body/eval_jaxpr/ppermute | solution.py:15
  204.6 16.3 %collective-permute-start = (f32[32,64,128]{2,1,0:T(8,128)}, f32[32,64,128]{2,1,0:T(8,128)S(1)}, u32[]{:S(2)}, u32[]{:S(2)}) collective-permute-start(f32[32,64,128]{2,1,0:T(8,128)} %multiply_add_fusion.7), channel_id=1, source_target_pairs={{0,8},{8,16},{16,24},{1,9},{9,17},{17,25},{2,10},{10,18},{18,26},{... | collective-permute-start | bytes 3145736 | tf_op jit(solution)/shard_map/while/body/eval_jaxpr/ppermute | solution.py:15
  267.6 15.6 %collective-permute-start.1 = (bf16[32,64,128]{2,1,0:T(8,128)(2,1)}, bf16[32,64,128]{2,1,0:T(8,128)(2,1)}, u32[]{:S(2)}, u32[]{:S(2)}) collective-permute-start(bf16[32,64,128]{2,1,0:T(8,128)(2,1)} %fusion.132), channel_id=1, source_target_pairs={{8,0},{16,8},{24,16},{9,1},{17,9},{25,17},{10,2},{18,10},{26,18},{... | collective-permute-start | bytes 1572872 | tf_op jit(solution)/shard_map/while/body/eval_jaxpr/ppermute | solution.py:15
  287.9 11.4 %collective-permute-start.1 = (bf16[32,64,128]{2,1,0:T(8,128)(2,1)}, bf16[32,64,128]{2,1,0:T(8,128)(2,1)}, u32[]{:S(2)}, u32[]{:S(2)}) collective-permute-start(bf16[32,64,128]{2,1,0:T(8,128)(2,1)} %fusion.132), channel_id=1, source_target_pairs={{8,0},{16,8},{24,16},{9,1},{17,9},{25,17},{10,2},{18,10},{26,18},{... | collective-permute-start | bytes 1572872 | tf_op jit(solution)/shard_map/while/body/eval_jaxpr/ppermute | solution.py:15
  304.0 10.8 %collective-permute-start.1 = (bf16[32,64,128]{2,1,0:T(8,128)(2,1)}, bf16[32,64,128]{2,1,0:T(8,128)(2,1)}, u32[]{:S(2)}, u32[]{:S(2)}) collective-permute-start(bf16[32,64,128]{2,1,0:T(8,128)(2,1)} %fusion.132), channel_id=1, source_target_pairs={{8,0},{16,8},{24,16},{9,1},{17,9},{25,17},{10,2},{18,10},{26,18},{... | collective-permute-start | bytes 1572872 | tf_op jit(solution)/shard_map/while/body/eval_jaxpr/ppermute | solution.py:15
  383.4 9.9 %collective-permute-start.3 = (f32[3,2304]{1,0:T(4,128)S(1)}, f32[3,2304]{1,0:T(4,128)S(1)}, u32[]{:S(2)}, u32[]{:S(2)}) collective-permute-start(f32[3,2304]{1,0:T(4,128)S(1)} %pad_add_fusion.1), channel_id=1, source_target_pairs={{8,0},{16,8},{24,16},{9,1},{17,9},{25,17},{10,2},{18,10},{26,18},{... | collective-permute-start | bytes 82952 | tf_op jit(solution)/shard_map/ppermute | solution.py:15
  412.3 251.1 %reduce-scatter.5.cloned.1.call-start = ((), (), s32[]{:S(2)}) async-start(), calls=%async_computation.4 | async-start | bytes 4718592 | tf_op jit(solution)/shard_map/reduce_scatter | solution.py:203
  417.5 303.6 %all-reduce.18.cloned.1.call-start = ((), (), s32[]{:S(2)}) async-start(), calls=%async_computation.6 | async-start | bytes 3293184 | tf_op jit(solution)/shard_map/psum | solution.py:207
  423.1 240.3 %copy-start.23 = (bf16[1,256,1024]{2,1,0:T(8,128)(2,1)S(1)}, bf16[1,256,1024]{2,1,0:T(8,128)(2,1)}, u32[]{:S(2)}) copy-start(bf16[1,256,1024]{2,1,0:T(8,128)(2,1)} %param.15) | copy-start | bytes 1572868
  423.1 240.3 %copy-start.25 = (bf16[253,2304]{1,0:T(8,128)(2,1)S(1)}, bf16[253,2304]{1,0:T(8,128)(2,1)}, u32[]{:S(2)}) copy-start(bf16[253,2304]{1,0:T(8,128)(2,1)} %copy-done.24) | copy-start | bytes 3497476
  (60 other events, 255.0 us)
Sparse Core Ops, SparseCore 0:
  10.1 134.8 all-gather.2
  147.1 70.9 all-gather.4
  412.4 159.9 reduce-scatter.6
  575.9 87.3 reduce-scatter.4
  666.2 43.9 all-reduce.17
